TPU v7x, 256 devices: a whole 4x4x8 slice. The times are simulated.
256 devices in a mesh: px: 32 (over z_lo, y, x), py: 8 (over z_hi, core).
Axes of the slice: x: 4, y: 4, z: 8 (z_hi: 4, z_lo: 2; z = z_hi * 2 + z_lo), core: 2. Of those that a mesh axis runs over, the one named last changes fastest.
Arguments:
- log_source: float32 [256, 256, 256], P('px', 'py'), may hold values from -12 to 240, as said below
- log_target: float32 [256, 256, 256], P('px', 'py'), may hold values from -12 to 240, as said below
Outputs:
- potential_f: float32 [256, 256, 256], P('px', 'py')
- potential_g: float32 [256, 256, 256], P('px', 'py')
Inputs may be any that keep to these rules, and one draw needn't show every extreme that they name: `log_source`: Log-density values on every cell. `log_target`: Log-density values on every cell.
All inputs are finite; a program needn't handle non-finite values.
Results may differ from a plain program's by a relative error of at most 0.0001.
Values sent between devices are 32-bit elements; how exact they have to be, the bound alone decides.
A program may use at most 128 MiB of HBM per device.

v0:
```python
from functools import partial
import math
import jax
import jax.numpy as jnp
from jax import lax
from jax.sharding import PartitionSpec as P

LEVELS = 3
ITERS = 2
FINE_ITERS = 1
BAND = 16


def epsilon_of(level_index):
    return 0.05 * 2.0 ** (LEVELS - 1 - level_index)


def soft_axis(values, along, level_index):
    inverse_width = 2.0 ** (LEVELS - 1 - level_index) / 18.0
    window = [1, 1, 1]
    window[along] = 2 * BAND + 1
    padding = [(0, 0), (0, 0), (0, 0)]
    padding[along] = (BAND, BAND)
    line_max = lax.reduce_window(
        values, -jnp.inf, lax.max, tuple(window), (1, 1, 1), tuple(padding)
    )
    padded = jnp.pad(values, padding, constant_values=-jnp.inf)
    length = values.shape[along]
    summed = jnp.zeros_like(values)
    for offset in range(2 * BAND + 1):
        shifted = lax.slice_in_dim(padded, offset, offset + length, axis=along)
        weight = math.exp(-float((offset - BAND) ** 2) * inverse_width)
        summed = summed + weight * jnp.exp(shifted - line_max)
    return line_max + jnp.log(summed)


def restrict(values):
    size_a, size_b, size_c = values.shape
    blocks = values.reshape(size_a // 2, 2, size_b // 2, 2, size_c // 2, 2)
    block_max = jnp.max(blocks, axis=(1, 3, 5), keepdims=True)
    merged = block_max + jnp.log(
        jnp.mean(jnp.exp(blocks - block_max), axis=(1, 3, 5), keepdims=True)
    )
    return merged.reshape(size_a // 2, size_b // 2, size_c // 2)


def prolong(values):
    return jnp.repeat(jnp.repeat(jnp.repeat(values, 2, axis=0), 2, axis=1), 2, axis=2)


def unchanged(values):
    return values


def forward(values, rows_fn, columns_fn):
    middle = rows_fn(lax.all_to_all(values, "py", split_axis=2, concat_axis=1, tiled=True))
    return columns_fn(lax.all_to_all(middle, "px", split_axis=1, concat_axis=0, tiled=True))


def backward(values, rows_fn, depth_fn):
    middle = rows_fn(lax.all_to_all(values, "px", split_axis=0, concat_axis=1, tiled=True))
    return depth_fn(lax.all_to_all(middle, "py", split_axis=1, concat_axis=2, tiled=True))


def pencil_level(level_index, source_level, target_level, potential_g):
    epsilon = epsilon_of(level_index)
    sweeps = FINE_ITERS if level_index == LEVELS - 1 else ITERS
    along_first = partial(soft_axis, along=0, level_index=level_index)
    along_second = partial(soft_axis, along=1, level_index=level_index)
    along_third = partial(soft_axis, along=2, level_index=level_index)
    potential_f = potential_g
    source_turned = forward(source_level, unchanged, unchanged)
    turned_f = source_turned
    for iteration in range(sweeps):
        reached = forward(along_third(potential_g / epsilon), along_second, along_first)
        turned_f = epsilon * (source_turned - reached)
        pulled = backward(along_first(turned_f / epsilon), along_second, along_third)
        potential_g = epsilon * (target_level - pulled)
    if level_index == LEVELS - 1:
        potential_f = backward(turned_f, unchanged, unchanged)
    return (potential_f, potential_g)


def per_device(log_source, log_target):
    sources = [log_source]
    targets = [log_target]
    for level_index in range(LEVELS - 1):
        sources = sources + [restrict(sources[-1])]
        targets = targets + [restrict(targets[-1])]
    sources = sources[::-1]
    targets = targets[::-1]
    potential_g = jnp.zeros_like(sources[0])
    potential_f = potential_g
    first_level = 0
    for level_index in range(first_level, LEVELS):
        potential_f, potential_g = pencil_level(
            level_index, sources[level_index], targets[level_index], potential_g
        )
        if level_index < LEVELS - 1:
            potential_g = prolong(potential_g)
    return (potential_f, potential_g)


def solution(mesh):
    return jax.shard_map(
        per_device,
        mesh=mesh,
        in_specs=(P("px", "py", None), P("px", "py", None)),
        out_specs=(P("px", "py", None), P("px", "py", None)),
        check_vma=False,
    )
```

profile of v0, /device:TPU:1, one launch (start us, length us, event | category | flops | bytes accessed | tf_op | source)
XLA Modules:
  0.0 639.6 jit_solution(10024164577190180262)
XLA Ops:
  0.6 18.9 %reshape.69 = f32[4,2,16,2,128,2]{5,4,3,2,1,0:T(8,128)} reshape(f32[8,32,256]{2,1,0:T(8,128)} %param.2) | data formatting | bytes 524288 | tf_op jit(solution)/shard_map/reshape | solution.py:39
  19.5 7.0 %reduce_max.37 = f32[4,16,128]{2,1,0:T(8,128)S(1)} reduce(f32[4,2,16,2,128,2]{5,4,3,2,1,0:T(8,128)} %reshape.69, f32[]{:T(128)} %constant.46.clone.1), dimensions={1,3,5}, to_apply=%region_2.0 | reduce | flops 57344 | bytes 294916 | tf_op jit(solution)/shard_map/reduce_max | solution.py:40
  26.5 8.2 %exponential_reduce_fusion = f32[4,16,128]{2,1,0:T(8,128)S(1)} fusion(f32[4,2,16,2,128,2]{5,4,3,2,1,0:T(8,128)} %reshape.69, f32[4,16,128]{2,1,0:T(8,128)S(1)} %reduce_max.37), kind=kLoop, calls=%fused_computation | loop fusion | flops 122880 | bytes 327680 | tf_op jit(solution)/shard_map/reduce_sum | solution.py:42
  38.5 10.0 %all-to-all-start.4 = ((f32[8,1,128]{2,1,0:T(1,128)}), f32[8,1,128]{2,1,0:T(1,128)S(1)}, u32[]{:S(2)}, u32[]{:S(2)}) async-start(f32[8,1,128]{2,1,0:T(1,128)} %reshape.78), calls=%async_computation.4 | async-start | bytes 8192 | tf_op jit(solution)/shard_map/all_to_all | solution.py:56
  49.5 5.9 all-to-all-done.4
  55.4 3.9 all-to-all-start.6
  59.3 18.1 %reshape.68 = f32[4,2,16,2,128,2]{5,4,3,2,1,0:T(8,128)} reshape(f32[8,32,256]{2,1,0:T(8,128)S(1)} %copy-done.1) | data formatting | bytes 524288 | tf_op jit(solution)/shard_map/reshape | solution.py:39
  77.4 7.0 %reduce_max.36 = f32[4,16,128]{2,1,0:T(8,128)S(1)} reduce(f32[4,2,16,2,128,2]{5,4,3,2,1,0:T(8,128)} %reshape.68, f32[]{:T(128)} %constant.46.clone.1), dimensions={1,3,5}, to_apply=%region_0.0 | reduce | flops 57344 | bytes 294916 | tf_op jit(solution)/shard_map/reduce_max | solution.py:40
  86.4 7.5 %all-to-all-start.5 = ((f32[2,64,8]{2,0,1:T(2,128)}), f32[2,64,8]{2,0,1:T(2,128)S(1)}, u32[]{:S(2)}, u32[]{:S(2)}) async-start(f32[2,64,8]{2,0,1:T(2,128)} %bitcast.15), calls=%async_computation.5 | async-start | bytes 131072 | tf_op jit(solution)/shard_map/all_to_all | solution.py:57
  96.3 5.0 all-to-all-done.5
  101.3 4.1 all-to-all-start.7
  105.4 8.2 %exponential_reduce_fusion.1 = f32[4,16,128]{2,1,0:T(8,128)S(1)} fusion(f32[4,2,16,2,128,2]{5,4,3,2,1,0:T(8,128)} %reshape.68, f32[4,16,128]{2,1,0:T(8,128)S(1)} %reduce_max.36), kind=kLoop, calls=%fused_computation.1 | loop fusion | flops 122880 | bytes 327680 | tf_op jit(solution)/shard_map/reduce_sum | solution.py:42
  113.9 3.5 bitcast_subtract_fusion.4
  117.6 4.0 log_add_fusion.10
  121.6 7.9 %all-to-all-start.8 = ((f32[64,2,8]{2,1,0:T(2,128)}), f32[64,2,8]{2,1,0:T(2,128)S(1)}, u32[]{:S(2)}, u32[]{:S(2)}) async-start(f32[64,2,8]{2,1,0:T(2,128)} %log_add_fusion.10), calls=%async_computation.8 | async-start | bytes 131072 | tf_op jit(solution)/shard_map/all_to_all | solution.py:61
  131.8 4.8 all-to-all-done.8
  138.4 10.1 %all-to-all-start.9 = ((f32[8,1,128]{2,1,0:T(1,128)}), f32[8,1,128]{2,1,0:T(1,128)S(1)}, u32[]{:S(2)}, u32[]{:S(2)}) async-start(f32[8,1,128]{2,1,0:T(1,128)} %reshape.82), calls=%async_computation.9 | async-start | bytes 8192 | tf_op jit(solution)/shard_map/all_to_all | solution.py:62
  149.1 6.3 all-to-all-done.9
  158.2 10.1 %all_to_all.504 = f32[8,1,128]{2,1,0:T(1,128)S(1)} all-to-all(f32[8,1,128]{2,1,0:T(1,128)S(1)} %reshape.84), channel_id=1, replica_groups=mesh['px'=32,'py'=8] {'py'}, dimensions={0} | all-to-all | bytes 8192 | tf_op jit(solution)/shard_map/all_to_all | solution.py:56
  170.1 10.8 %all_to_all.505 = f32[2,64,8]{2,0,1:T(2,128)S(1)} all-to-all(f32[2,64,8]{2,0,1:T(2,128)S(1)} %copy.127), channel_id=1, replica_groups=mesh['px'=32,'py'=8] {'px'}, dimensions={1} | all-to-all | bytes 8192 | tf_op jit(solution)/shard_map/all_to_all | solution.py:57
  181.1 3.5 bitcast_subtract_fusion.3
  184.8 3.4 log_add_fusion.7
  188.2 10.6 %all_to_all.506 = f32[64,2,8]{2,1,0:T(2,128)S(1)} all-to-all(f32[64,2,8]{2,1,0:T(2,128)S(1)} %log_add_fusion.7), channel_id=1, replica_groups=mesh['px'=32,'py'=8] {'px'}, dimensions={0} | all-to-all | bytes 8192 | tf_op jit(solution)/shard_map/all_to_all | solution.py:61
  200.5 6.5 %all-to-all-start.13 = ((f32[8,1,128]{2,1,0:T(1,128)}), f32[8,1,128]{2,1,0:T(1,128)S(1)}, u32[]{:S(2)}, u32[]{:S(2)}) async-start(f32[8,1,128]{2,1,0:T(1,128)} %reshape.86), calls=%async_computation.13 | async-start | bytes 8192 | tf_op jit(solution)/shard_map/all_to_all | solution.py:62
  208.0 6.0 all-to-all-done.13
  214.0 3.9 all-to-all-start.2
  225.1 5.9 all-to-all-start.14
  233.0 5.1 all-to-all-done.14
  238.1 4.0 all-to-all-start.3
  249.3 6.7 %all-to-all-start.15 = ((f32[32,1,256]{2,1,0:T(1,128)}), f32[32,1,256]{2,1,0:T(1,128)S(1)}, u32[]{:S(2)}, u32[]{:S(2)}) async-start(f32[32,1,256]{2,1,0:T(1,128)} %reshape.90), calls=%async_computation.15 | async-start | bytes 65536 | tf_op jit(solution)/shard_map/all_to_all | solution.py:57
  256.9 6.2 all-to-all-done.15
  264.6 6.3 bitcast_subtract_fusion.2
  271.3 6.2 log_add_fusion.5
  277.8 10.7 %all_to_all.507 = f32[32,1,256]{2,1,0:T(1,128)S(1)} all-to-all(f32[32,1,256]{2,1,0:T(1,128)S(1)} %reshape.92), channel_id=1, replica_groups=mesh['px'=32,'py'=8] {'px'}, dimensions={0} | all-to-all | bytes 65536 | tf_op jit(solution)/shard_map/all_to_all | solution.py:61
  293.7 13.1 %all_to_all.508 = f32[8,1,1024]{2,1,0:T(1,128)S(1)} all-to-all(f32[8,1,1024]{2,1,0:T(1,128)S(1)} %reshape.94), channel_id=1, replica_groups=mesh['px'=32,'py'=8] {'py'}, dimensions={0} | all-to-all | bytes 65536 | tf_op jit(solution)/shard_map/all_to_all | solution.py:62
  314.1 10.2 %all_to_all.509 = f32[8,1,1024]{2,1,0:T(1,128)S(1)} all-to-all(f32[8,1,1024]{2,1,0:T(1,128)S(1)} %reshape.96), channel_id=1, replica_groups=mesh['px'=32,'py'=8] {'py'}, dimensions={0} | all-to-all | bytes 65536 | tf_op jit(solution)/shard_map/all_to_all | solution.py:56
  329.7 11.0 %all_to_all.510 = f32[32,1,256]{2,1,0:T(1,128)S(1)} all-to-all(f32[32,1,256]{2,1,0:T(1,128)S(1)} %reshape.98), channel_id=1, replica_groups=mesh['px'=32,'py'=8] {'px'}, dimensions={0} | all-to-all | bytes 65536 | tf_op jit(solution)/shard_map/all_to_all | solution.py:57
  342.0 6.3 bitcast_subtract_fusion.1
  348.8 6.2 log_add_fusion.4
  355.3 10.5 %all_to_all.511 = f32[32,1,256]{2,1,0:T(1,128)S(1)} all-to-all(f32[32,1,256]{2,1,0:T(1,128)S(1)} %reshape.100), channel_id=1, replica_groups=mesh['px'=32,'py'=8] {'px'}, dimensions={0} | all-to-all | bytes 65536 | tf_op jit(solution)/shard_map/all_to_all | solution.py:61
  371.7 6.7 %all-to-all-start.21 = ((f32[8,1,1024]{2,1,0:T(1,128)}), f32[8,1,1024]{2,1,0:T(1,128)S(1)}, u32[]{:S(2)}, u32[]{:S(2)}) async-start(f32[8,1,1024]{2,1,0:T(1,128)} %reshape.102), calls=%async_computation.21 | async-start | bytes 65536 | tf_op jit(solution)/shard_map/all_to_all | solution.py:62
  379.9 5.6 all-to-all-done.21
  385.5 4.2 all-to-all-start
  394.5 9.6 %reduce_window_max.288 = f32[8,32,256]{2,1,0:T(8,128)S(1)} reduce-window(f32[8,32,256]{2,1,0:T(8,128)S(1)} %copy.152, f32[]{:T(128)} %constant.46.clone.1), window={size=1x1x33 pad=0_0x0_0x16_16}, to_apply=%region_31.32 | reduce-window | flops 2097152 | bytes 524292 | tf_op jit(solution)/shard_map/reduce_window_max | solution.py:24
  408.1 7.2 %all-to-all-start.22 = ((f32[8,1,8192]{2,1,0:T(1,128)}), f32[8,1,8192]{2,1,0:T(1,128)S(1)}, u32[]{:S(2)}, u32[]{:S(2)}) async-start(f32[8,1,8192]{2,1,0:T(1,128)} %reshape.104), calls=%async_computation.22 | async-start | bytes 524288 | tf_op jit(solution)/shard_map/all_to_all | solution.py:56
  418.4 7.0 %all-to-all-done.22 = f32[8,1,8192]{2,1,0:T(1,128)S(1)} async-done(((f32[8,1,8192]{2,1,0:T(1,128)}), f32[8,1,8192]{2,1,0:T(1,128)S(1)}, u32[]{:S(2)}, u32[]{:S(2)}) %all-to-all-start.22) | async-done | bytes 262176 | tf_op jit(solution)/shard_map/all_to_all | solution.py:56
  425.4 3.9 all-to-all-start.1
  431.3 18.9 %fusion.2788 = f32[8,256,32]{2,0,1:T(8,128)S(1)} fusion(f32[8,256,32]{2,0,1:T(8,128)S(1)} %bitcast.225), kind=kOutput, calls=%fused_computation.3558 | output fusion | flops 2097152 | bytes 524288 | tf_op jit(solution)/shard_map/reduce_window_max | solution.py:24
  450.1 11.8 %fusion.2778 = f32[256,8,32]{2,1,0:T(8,128)S(1)} fusion(f32[8,256,32]{2,0,1:T(8,128)S(1)} %fusion.2788, f32[8,256,32]{2,0,1:T(8,128)S(1)} %bitcast.226), kind=kLoop, calls=%fused_computation.3541 | loop fusion | flops 6422528 | bytes 786432
  463.1 7.8 %all-to-all-start.23 = ((f32[32,1,2048]{2,1,0:T(1,128)}), f32[32,1,2048]{2,1,0:T(1,128)S(1)}, u32[]{:S(2)}, u32[]{:S(2)}) async-start(f32[32,1,2048]{2,1,0:T(1,128)} %reshape.106), calls=%async_computation.23 | async-start | bytes 524288 | tf_op jit(solution)/shard_map/all_to_all | solution.py:57
  472.6 6.2 all-to-all-done.23
  480.5 18.9 %fusion.2789 = f32[256,8,32]{2,1,0:T(8,128)S(1)} fusion(f32[256,8,32]{2,1,0:T(8,128)S(1)} %bitcast.209), kind=kOutput, calls=%fused_computation.3559 | output fusion | flops 2097152 | bytes 524288 | tf_op jit(solution)/shard_map/reduce_window_max | solution.py:24
  499.4 11.9 %broadcast_multiply_fusion = (f32[256,8,32]{2,1,0:T(8,128)S(1)}, f32[256,8,32]{2,1,0:T(8,128)S(1)}) fusion(f32[256,8,32]{2,1,0:T(8,128)S(1)} %fusion.2789, f32[256,8,32]{2,1,0:T(8,128)S(1)} %bitcast.210, f32[32,8,8,32]{3,2,1,0:T(8,128)S(1)} %copy.107), kind=kLoop, calls=%fused_computation.802 | loop fusion | flops 6553600 | bytes 1310720 | tf_op jit(solution)/shard_map/mul | solution.py:76
  512.5 3.9 all-to-all-start.24
  516.4 18.9 %fusion.2790 = f32[256,8,32]{2,1,0:T(8,128)S(1)} fusion(f32[256,8,32]{2,1,0:T(8,128)S(1)} %get-tuple-element.3), kind=kOutput, calls=%fused_computation.3560 | output fusion | flops 2097152 | bytes 524288 | tf_op jit(solution)/shard_map/reduce_window_max | solution.py:24
  535.2 11.8 %log_add_fusion.1 = f32[256,8,32]{2,1,0:T(8,128)S(1)} fusion(f32[256,8,32]{2,1,0:T(8,128)S(1)} %fusion.2790, f32[256,8,32]{2,1,0:T(8,128)S(1)} %get-tuple-element.3), kind=kLoop, calls=%fused_computation.222 | loop fusion | flops 6422528 | bytes 786432 | tf_op jit(solution)/shard_map/add | solution.py:34
  548.2 7.8 %all-to-all-start.26 = ((f32[32,1,2048]{2,1,0:T(1,128)}), f32[32,1,2048]{2,1,0:T(1,128)S(1)}, u32[]{:S(2)}, u32[]{:S(2)}) async-start(f32[32,1,2048]{2,1,0:T(1,128)} %reshape.112), calls=%async_computation.26 | async-start | bytes 524288 | tf_op jit(solution)/shard_map/all_to_all | solution.py:61
  559.3 4.5 all-to-all-done.26
  563.8 9.3 %all-to-all-start.25 = ((f32[8,1,8192]{2,1,0:T(1,128)}), f32[8,1,8192]{2,1,0:T(1,128)S(1)}, u32[]{:S(2)}, u32[]{:S(2)}) async-start(f32[8,1,8192]{2,1,0:T(1,128)} %reshape.110), calls=%async_computation.25 | async-start | bytes 524288 | tf_op jit(solution)/shard_map/all_to_all | solution.py:62
  574.9 18.9 %fusion.2791 = f32[8,256,32]{2,0,1:T(8,128)S(1)} fusion(f32[8,256,32]{2,0,1:T(8,128)S(1)} %bitcast.227), kind=kOutput, calls=%fused_computation.3561 | output fusion | flops 2097152 | bytes 524288 | tf_op jit(solution)/shard_map/reduce_window_max | solution.py:24
  593.8 11.8 %fusion.2779 = f32[256,8,32]{2,1,0:T(8,128)S(1)} fusion(f32[8,256,32]{2,0,1:T(8,128)S(1)} %fusion.2791, f32[8,256,32]{2,0,1:T(8,128)S(1)} %bitcast.228), kind=kLoop, calls=%fused_computation.3542 | loop fusion | flops 6422528 | bytes 786432
  606.7 7.2 %all-to-all-start.27 = ((f32[8,1,8192]{2,1,0:T(1,128)}), f32[8,1,8192]{2,1,0:T(1,128)S(1)}, u32[]{:S(2)}, u32[]{:S(2)}) async-start(f32[8,1,8192]{2,1,0:T(1,128)} %reshape.114), calls=%async_computation.27 | async-start | bytes 524288 | tf_op jit(solution)/shard_map/all_to_all | solution.py:62
  617.1 6.9 %all-to-all-done.27 = f32[8,1,8192]{2,1,0:T(1,128)S(1)} async-done(((f32[8,1,8192]{2,1,0:T(1,128)}), f32[8,1,8192]{2,1,0:T(1,128)S(1)}, u32[]{:S(2)}, u32[]{:S(2)}) %all-to-all-start.27) | async-done | bytes 262176 | tf_op jit(solution)/shard_map/all_to_all | solution.py:62
  626.5 9.6 %reduce_window_max.293 = f32[8,32,256]{2,1,0:T(8,128)S(1)} reduce-window(f32[8,32,256]{2,1,0:T(8,128)S(1)} %all_to_all.475, f32[]{:T(128)} %constant.46.clone.1), window={size=1x1x33 pad=0_0x0_0x16_16}, to_apply=%region_36.37 | reduce-window | flops 2097152 | bytes 524292 | tf_op jit(solution)/shard_map/reduce_window_max | solution.py:24
  (199 shorter events, 103.5 us)
Async XLA Ops:
  36.8 22.5 %copy-start.1 = (f32[8,32,256]{2,1,0:T(8,128)S(1)}, f32[8,32,256]{2,1,0:T(8,128)}, u32[]{:S(2)}) copy-start(f32[8,32,256]{2,1,0:T(8,128)} %param.3) | copy-start | bytes 786436
  38.5 16.9 %all-to-all-start.4 = ((f32[8,1,128]{2,1,0:T(1,128)}), f32[8,1,128]{2,1,0:T(1,128)S(1)}, u32[]{:S(2)}, u32[]{:S(2)}) async-start(f32[8,1,128]{2,1,0:T(1,128)} %reshape.78), calls=%async_computation.4 | async-start | bytes 8192 | tf_op jit(solution)/shard_map/all_to_all | solution.py:56
  55.4 31.0 %all-to-all-start.6 = ((f32[8,1,128]{2,1,0:T(1,128)}), f32[8,1,128]{2,1,0:T(1,128)S(1)}, u32[]{:S(2)}, u32[]{:S(2)}) async-start(f32[8,1,128]{2,1,0:T(1,128)} %reshape.80), calls=%async_computation.6 | async-start | bytes 8192 | tf_op jit(solution)/shard_map/all_to_all | solution.py:56
  86.4 14.9 %all-to-all-start.5 = ((f32[2,64,8]{2,0,1:T(2,128)}), f32[2,64,8]{2,0,1:T(2,128)S(1)}, u32[]{:S(2)}, u32[]{:S(2)}) async-start(f32[2,64,8]{2,0,1:T(2,128)} %bitcast.15), calls=%async_computation.5 | async-start | bytes 131072 | tf_op jit(solution)/shard_map/all_to_all | solution.py:57
  101.3 12.3 %all-to-all-start.7 = ((f32[2,64,8]{2,0,1:T(2,128)}), f32[2,64,8]{2,0,1:T(2,128)S(1)}, u32[]{:S(2)}, u32[]{:S(2)}) async-start(f32[2,64,8]{2,0,1:T(2,128)} %copy.120), calls=%async_computation.7 | async-start | bytes 131072 | tf_op jit(solution)/shard_map/all_to_all | solution.py:57
  121.6 15.1 %all-to-all-start.8 = ((f32[64,2,8]{2,1,0:T(2,128)}), f32[64,2,8]{2,1,0:T(2,128)S(1)}, u32[]{:S(2)}, u32[]{:S(2)}) async-start(f32[64,2,8]{2,1,0:T(2,128)} %log_add_fusion.10), calls=%async_computation.8 | async-start | bytes 131072 | tf_op jit(solution)/shard_map/all_to_all | solution.py:61
  138.4 17.1 %all-to-all-start.9 = ((f32[8,1,128]{2,1,0:T(1,128)}), f32[8,1,128]{2,1,0:T(1,128)S(1)}, u32[]{:S(2)}, u32[]{:S(2)}) async-start(f32[8,1,128]{2,1,0:T(1,128)} %reshape.82), calls=%async_computation.9 | async-start | bytes 8192 | tf_op jit(solution)/shard_map/all_to_all | solution.py:62
  200.5 13.4 %all-to-all-start.13 = ((f32[8,1,128]{2,1,0:T(1,128)}), f32[8,1,128]{2,1,0:T(1,128)S(1)}, u32[]{:S(2)}, u32[]{:S(2)}) async-start(f32[8,1,128]{2,1,0:T(1,128)} %reshape.86), calls=%async_computation.13 | async-start | bytes 8192 | tf_op jit(solution)/shard_map/all_to_all | solution.py:62
  214.0 11.1 %all-to-all-start.2 = ((f32[8,1,1024]{2,1,0:T(1,128)}), f32[8,1,1024]{2,1,0:T(1,128)S(1)}, u32[]{:S(2)}, u32[]{:S(2)}) async-start(f32[8,1,1024]{2,1,0:T(1,128)} %reshape.74), calls=%async_computation.2 | async-start | bytes 65536 | tf_op jit(solution)/shard_map/all_to_all | solution.py:56
  225.1 13.0 %all-to-all-start.14 = ((f32[8,1,1024]{2,1,0:T(1,128)}), f32[8,1,1024]{2,1,0:T(1,128)S(1)}, u32[]{:S(2)}, u32[]{:S(2)}) async-start(f32[8,1,1024]{2,1,0:T(1,128)} %reshape.88), calls=%async_computation.14 | async-start | bytes 65536 | tf_op jit(solution)/shard_map/all_to_all | solution.py:56
  238.1 11.2 %all-to-all-start.3 = ((f32[32,1,256]{2,1,0:T(1,128)}), f32[32,1,256]{2,1,0:T(1,128)S(1)}, u32[]{:S(2)}, u32[]{:S(2)}) async-start(f32[32,1,256]{2,1,0:T(1,128)} %reshape.76), calls=%async_computation.3 | async-start | bytes 65536 | tf_op jit(solution)/shard_map/all_to_all | solution.py:57
  249.3 13.9 %all-to-all-start.15 = ((f32[32,1,256]{2,1,0:T(1,128)}), f32[32,1,256]{2,1,0:T(1,128)S(1)}, u32[]{:S(2)}, u32[]{:S(2)}) async-start(f32[32,1,256]{2,1,0:T(1,128)} %reshape.90), calls=%async_computation.15 | async-start | bytes 65536 | tf_op jit(solution)/shard_map/all_to_all | solution.py:57
  348.8 29.5 %copy-start = (f32[8,32,256]{2,1,0:T(8,128)S(1)}, f32[8,32,256]{2,1,0:T(8,128)}, u32[]{:S(2)}) copy-start(f32[8,32,256]{2,1,0:T(8,128)} %param.2) | copy-start | bytes 786436
  371.7 13.8 %all-to-all-start.21 = ((f32[8,1,1024]{2,1,0:T(1,128)}), f32[8,1,1024]{2,1,0:T(1,128)S(1)}, u32[]{:S(2)}, u32[]{:S(2)}) async-start(f32[8,1,1024]{2,1,0:T(1,128)} %reshape.102), calls=%async_computation.21 | async-start | bytes 65536 | tf_op jit(solution)/shard_map/all_to_all | solution.py:62
  385.5 22.6 %all-to-all-start = ((f32[8,1,8192]{2,1,0:T(1,128)}), f32[8,1,8192]{2,1,0:T(1,128)S(1)}, u32[]{:S(2)}, u32[]{:S(2)}) async-start(f32[8,1,8192]{2,1,0:T(1,128)} %reshape.70), calls=%async_computation | async-start | bytes 524288 | tf_op jit(solution)/shard_map/all_to_all | solution.py:56
  408.1 17.3 %all-to-all-start.22 = ((f32[8,1,8192]{2,1,0:T(1,128)}), f32[8,1,8192]{2,1,0:T(1,128)S(1)}, u32[]{:S(2)}, u32[]{:S(2)}) async-start(f32[8,1,8192]{2,1,0:T(1,128)} %reshape.104), calls=%async_computation.22 | async-start | bytes 524288 | tf_op jit(solution)/shard_map/all_to_all | solution.py:56
  425.4 37.7 %all-to-all-start.1 = ((f32[32,1,2048]{2,1,0:T(1,128)}), f32[32,1,2048]{2,1,0:T(1,128)S(1)}, u32[]{:S(2)}, u32[]{:S(2)}) async-start(f32[32,1,2048]{2,1,0:T(1,128)} %reshape.72), calls=%async_computation.1 | async-start | bytes 524288 | tf_op jit(solution)/shard_map/all_to_all | solution.py:57
  463.1 15.7 %all-to-all-start.23 = ((f32[32,1,2048]{2,1,0:T(1,128)}), f32[32,1,2048]{2,1,0:T(1,128)S(1)}, u32[]{:S(2)}, u32[]{:S(2)}) async-start(f32[32,1,2048]{2,1,0:T(1,128)} %reshape.106), calls=%async_computation.23 | async-start | bytes 524288 | tf_op jit(solution)/shard_map/all_to_all | solution.py:57
  512.5 35.7 %all-to-all-start.24 = ((f32[32,1,2048]{2,1,0:T(1,128)}), f32[32,1,2048]{2,1,0:T(1,128)S(1)}, u32[]{:S(2)}, u32[]{:S(2)}) async-start(f32[32,1,2048]{2,1,0:T(1,128)} %reshape.108), calls=%async_computation.24 | async-start | bytes 524288 | tf_op jit(solution)/shard_map/all_to_all | solution.py:61
  548.2 15.7 %all-to-all-start.26 = ((f32[32,1,2048]{2,1,0:T(1,128)}), f32[32,1,2048]{2,1,0:T(1,128)S(1)}, u32[]{:S(2)}, u32[]{:S(2)}) async-start(f32[32,1,2048]{2,1,0:T(1,128)} %reshape.112), calls=%async_computation.26 | async-start | bytes 524288 | tf_op jit(solution)/shard_map/all_to_all | solution.py:61
  563.8 42.9 %all-to-all-start.25 = ((f32[8,1,8192]{2,1,0:T(1,128)}), f32[8,1,8192]{2,1,0:T(1,128)S(1)}, u32[]{:S(2)}, u32[]{:S(2)}) async-start(f32[8,1,8192]{2,1,0:T(1,128)} %reshape.110), calls=%async_computation.25 | async-start | bytes 524288 | tf_op jit(solution)/shard_map/all_to_all | solution.py:62
  606.7 17.3 %all-to-all-start.27 = ((f32[8,1,8192]{2,1,0:T(1,128)}), f32[8,1,8192]{2,1,0:T(1,128)S(1)}, u32[]{:S(2)}, u32[]{:S(2)}) async-start(f32[8,1,8192]{2,1,0:T(1,128)} %reshape.114), calls=%async_computation.27 | async-start | bytes 524288 | tf_op jit(solution)/shard_map/all_to_all | solution.py:62
where the time goes:
time: 650 us; the launch traced here: 640 us
  other arithmetic  273 us (42%)
  starting transfers between devices  128 us (20%)
  blocking collectives  87 us (13%)
  local copies, waits for them, and re-layouts  76.4 us (12%)
  waiting for transfers between devices  72.1 us (11%)
    another operation x29, other arithmetic, soft_axis(): lax.reduce_window(values, -jnp.inf, lax.max, tuple(window), (1, 1, 1), tu...  119 us
    add x17, other arithmetic, soft_axis(): return line_max + jnp.log(summed)  44.7 us
    all_to_all x5, starting transfers between devices, backward(): lax.all_to_all(middle, 'py', split_axis=1, concat_axis=2, tiled=True)  39.8 us
    reshape x2, local copies, waits for them, and re-layouts, restrict(): blocks = values.reshape(size_a // 2, 2, size_b // 2, 2, size_c // 2, 2)  36.9 us
    all_to_all x6, starting transfers between devices, forward(): lax.all_to_all(values, 'py', split_axis=2, concat_axis=1, tiled=True)  35.2 us
    all_to_all x6, starting transfers between devices, forward(): lax.all_to_all(middle, 'px', split_axis=1, concat_axis=0, tiled=True)  33.9 us
    all_to_all x3, blocking collectives, backward(): lax.all_to_all(values, 'px', split_axis=0, concat_axis=1, tiled=True)  31.9 us
    all_to_all x5, waiting for transfers between devices, backward(): lax.all_to_all(middle, 'py', split_axis=1, concat_axis=2, tiled=True)  24.8 us
  transfers between devices with their start and end apart: 20, of which 14 were waited for; matrix products, arithmetic and copies ran while one was open for 29% of the time, Pallas kernels for 0%

commit v1 on v0

--- a/solution.py
+++ b/solution.py
@@ -54,7 +54,12 @@
 
 def forward(values, rows_fn, columns_fn):
     middle = rows_fn(lax.all_to_all(values, "py", split_axis=2, concat_axis=1, tiled=True))
-    return columns_fn(lax.all_to_all(middle, "px", split_axis=1, concat_axis=0, tiled=True))
+    return columns_fn(
+        jnp.concatenate(
+            lax.all_to_all(jnp.stack(jnp.split(middle, lax.axis_size("px"), axis=1)), "px", 0, 0),
+            axis=0,
+        )
+    )
 
 
 def backward(values, rows_fn, depth_fn):

time: 650 us -> 699 us (1.075)
  local copies, waits for them, and re-layouts: 76.4 us -> 118 us
  blocking collectives: 87 us -> 54.9 us
  waiting for transfers between devices: 72.1 us -> 95.9 us
  starting transfers between devices: 128 us -> 139 us
    unnamed x52 -> x304, local copies, waits for them, and re-layouts: 23.7 us -> 64.6 us
    all_to_all x3 -> x1, blocking collectives: 31.9 us -> 10.7 us  [backward(): lax.all_to_all(values, 'px', split_axis=0, concat_axis=1, tiled=True)]
    all_to_all x6 -> x7, waiting for transfers between devices: 18.6 us -> 32.4 us  [forward(): lax.all_to_all(jnp.stack(jnp.split(middle, lax.axis_size('px'), axis=1)),...]
    add x17 -> x18, other arithmetic: 44.7 us -> 57.7 us  [soft_axis(): return line_max + jnp.log(summed)]
    unnamed x2 -> x1, other arithmetic: 23.5 us -> 11.8 us
    all_to_all x2 -> x1, blocking collectives: 21.8 us -> 10.8 us  [forward(): lax.all_to_all(jnp.stack(jnp.split(middle, lax.axis_size('px'), axis=1)),...]
    all_to_all x3 -> x5, waiting for transfers between devices: 9.37 us -> 20.1 us  [backward(): lax.all_to_all(values, 'px', split_axis=0, concat_axis=1, tiled=True)]
    all_to_all x6 -> x7, starting transfers between devices: 33.9 us -> 38.2 us  [forward(): lax.all_to_all(jnp.stack(jnp.split(middle, lax.axis_size('px'), axis=1)),...]
  transfers between devices with their start and end apart: 20 -> 23, of which waited for: 14 -> 17; matrix products, arithmetic and copies ran while one was open for 29% -> 29% of each run, Pallas kernels for 0% -> 0%
where the time goes in v1:
time: 699 us; the launch traced here: 688 us
  other arithmetic  277 us (40%)
  starting transfers between devices  139 us (20%)
  local copies, waits for them, and re-layouts  118 us (17%)
  waiting for transfers between devices  95.9 us (14%)
  blocking collectives  54.9 us (8%)
    another operation x29, other arithmetic, soft_axis(): lax.reduce_window(values, -jnp.inf, lax.max, tuple(window), (1, 1, 1), tu...  119 us
    unnamed x304, local copies, waits for them, and re-layouts  64.6 us
    add x18, other arithmetic, soft_axis(): return line_max + jnp.log(summed)  57.7 us
    all_to_all x5, starting transfers between devices, backward(): lax.all_to_all(middle, 'py', split_axis=1, concat_axis=2, tiled=True)  39.8 us
    all_to_all x7, starting transfers between devices, forward(): lax.all_to_all(jnp.stack(jnp.split(middle, lax.axis_size('px'), axis=1)),...  38.2 us
    all_to_all x6, starting transfers between devices, forward(): lax.all_to_all(values, 'py', split_axis=2, concat_axis=1, tiled=True)  37.3 us
    reshape x2, local copies, waits for them, and re-layouts, restrict(): blocks = values.reshape(size_a // 2, 2, size_b // 2, 2, size_c // 2, 2)  36.9 us
    all_to_all x7, waiting for transfers between devices, forward(): lax.all_to_all(jnp.stack(jnp.split(middle, lax.axis_size('px'), axis=1)),...  32.4 us
  transfers between devices with their start and end apart: 23, of which 17 were waited for; matrix products, arithmetic and copies ran while one was open for 29% of the time, Pallas kernels for 0%

profile of v1, /device:TPU:1, one launch (start us, length us, event | category | flops | bytes accessed | tf_op | source)
XLA Modules:
  0.0 688.3 jit_solution(9222823978520933384)
XLA Ops:
  0.6 18.9 %reshape.94 = f32[4,2,16,2,128,2]{5,4,3,2,1,0:T(8,128)} reshape(f32[8,32,256]{2,1,0:T(8,128)} %param.2) | data formatting | bytes 524288 | tf_op jit(solution)/shard_map/reshape | solution.py:39
  19.5 7.0 %reduce_max.37 = f32[4,16,128]{2,1,0:T(8,128)S(1)} reduce(f32[4,2,16,2,128,2]{5,4,3,2,1,0:T(8,128)} %reshape.94, f32[]{:T(128)} %constant.46.clone.1), dimensions={1,3,5}, to_apply=%region_2.0 | reduce | flops 57344 | bytes 294916 | tf_op jit(solution)/shard_map/reduce_max | solution.py:40
  26.5 8.2 %exponential_reduce_fusion = f32[4,16,128]{2,1,0:T(8,128)S(1)} fusion(f32[4,2,16,2,128,2]{5,4,3,2,1,0:T(8,128)} %reshape.94, f32[4,16,128]{2,1,0:T(8,128)S(1)} %reduce_max.37), kind=kLoop, calls=%fused_computation | loop fusion | flops 122880 | bytes 327680 | tf_op jit(solution)/shard_map/reduce_sum | solution.py:42
  38.5 10.0 %all-to-all-start.4 = ((f32[8,1,128]{2,1,0:T(1,128)}), f32[8,1,128]{2,1,0:T(1,128)S(1)}, u32[]{:S(2)}, u32[]{:S(2)}) async-start(f32[8,1,128]{2,1,0:T(1,128)} %reshape.110), calls=%async_computation.4 | async-start | bytes 8192 | tf_op jit(solution)/shard_map/all_to_all | solution.py:56
  48.5 18.1 %reshape.93 = f32[4,2,16,2,128,2]{5,4,3,2,1,0:T(8,128)} reshape(f32[8,32,256]{2,1,0:T(8,128)S(1)} %copy-done.3) | data formatting | bytes 524288 | tf_op jit(solution)/shard_map/reshape | solution.py:39
  66.6 7.0 %reduce_max.36 = f32[4,16,128]{2,1,0:T(8,128)S(1)} reduce(f32[4,2,16,2,128,2]{5,4,3,2,1,0:T(8,128)} %reshape.93, f32[]{:T(128)} %constant.46.clone.1), dimensions={1,3,5}, to_apply=%region_0.0 | reduce | flops 57344 | bytes 294916 | tf_op jit(solution)/shard_map/reduce_max | solution.py:40
  73.6 8.2 %exponential_reduce_fusion.1 = f32[4,16,128]{2,1,0:T(8,128)S(1)} fusion(f32[4,2,16,2,128,2]{5,4,3,2,1,0:T(8,128)} %reshape.93, f32[4,16,128]{2,1,0:T(8,128)S(1)} %reduce_max.36), kind=kLoop, calls=%fused_computation.1 | loop fusion | flops 122880 | bytes 327680 | tf_op jit(solution)/shard_map/reduce_sum | solution.py:42
  82.8 7.2 %all-to-all-start.6 = ((f32[8,1,128]{2,1,0:T(1,128)}), f32[8,1,128]{2,1,0:T(1,128)S(1)}, u32[]{:S(2)}, u32[]{:S(2)}) async-start(f32[8,1,128]{2,1,0:T(1,128)} %reshape.112), calls=%async_computation.6 | async-start | bytes 8192 | tf_op jit(solution)/shard_map/all_to_all | solution.py:56
  130.0 7.5 %all-to-all-start.7 = ((f32[32,2,2,8]{3,2,1,0:T(2,128)}), f32[32,2,2,8]{3,2,1,0:T(2,128)S(1)}, u32[]{:S(2)}, u32[]{:S(2)}) async-start(f32[32,2,2,8]{3,2,1,0:T(2,128)} %constant_dynamic-update-slice_fusion.96), calls=%async_computation.7 | async-start | bytes 131072 | tf_op jit(solution)/shard_map/all_to_all | solution.py:59
  138.1 6.7 all-to-all-done.7
  144.8 3.9 all-to-all-start.5
  148.8 7.0 %all-to-all-done.5 = f32[32,2,2,8]{3,2,1,0:T(2,128)S(1)} async-done(((f32[32,2,2,8]{3,2,1,0:T(2,128)}), f32[32,2,2,8]{3,2,1,0:T(2,128)S(1)}, u32[]{:S(2)}, u32[]{:S(2)}) %all-to-all-start.5) | async-done | bytes 4128 | tf_op jit(solution)/shard_map/all_to_all | solution.py:59
  159.4 4.0 log_add_fusion.10
  163.4 3.9 all-to-all-start.8
  169.6 4.8 all-to-all-done.8
  176.2 10.8 %all-to-all-start.9 = ((f32[8,1,128]{2,1,0:T(1,128)}), f32[8,1,128]{2,1,0:T(1,128)S(1)}, u32[]{:S(2)}, u32[]{:S(2)}) async-start(f32[8,1,128]{2,1,0:T(1,128)} %reshape.114), calls=%async_computation.9 | async-start | bytes 8192 | tf_op jit(solution)/shard_map/all_to_all | solution.py:67
  187.7 6.3 all-to-all-done.9
  196.9 10.1 %all_to_all.400 = f32[8,1,128]{2,1,0:T(1,128)S(1)} all-to-all(f32[8,1,128]{2,1,0:T(1,128)S(1)} %reshape.116), channel_id=1, replica_groups=mesh['px'=32,'py'=8] {'py'}, dimensions={0} | all-to-all | bytes 8192 | tf_op jit(solution)/shard_map/all_to_all | solution.py:56
  209.3 10.8 %all_to_all.401 = f32[32,2,2,8]{3,2,1,0:T(2,128)S(1)} all-to-all(f32[32,2,2,8]{3,2,1,0:T(2,128)S(1)} %constant_dynamic-update-slice_fusion.128), channel_id=1, replica_groups=mesh['px'=32,'py'=8] {'px'}, dimensions={0} | all-to-all | bytes 8192 | tf_op jit(solution)/shard_map/all_to_all | solution.py:59
  223.9 4.0 log_add_fusion.7
  227.9 3.9 all-to-all-start.12
  232.7 6.2 all-to-all-done.12
  238.9 6.5 all-to-all-start.2
  247.2 5.4 all-to-all-done.2
  252.6 3.9 all-to-all-start.13
  269.5 3.9 all-to-all-start.14
  275.2 5.4 all-to-all-done.14
  280.6 4.0 all-to-all-start.3
  291.7 7.1 %all-to-all-start.15 = ((f32[32,1,256]{2,1,0:T(1,128)}), f32[32,1,256]{2,1,0:T(1,128)S(1)}, u32[]{:S(2)}, u32[]{:S(2)}) async-start(f32[32,1,256]{2,1,0:T(1,128)} %reshape.122), calls=%async_computation.15 | async-start | bytes 65536 | tf_op jit(solution)/shard_map/all_to_all | solution.py:59
  299.9 6.2 all-to-all-done.15
  307.5 6.3 bitcast_subtract_fusion.2
  314.3 6.2 log_add_fusion.5
  320.7 10.7 %all_to_all.402 = f32[32,1,256]{2,1,0:T(1,128)S(1)} all-to-all(f32[32,1,256]{2,1,0:T(1,128)S(1)} %reshape.124), channel_id=1, replica_groups=mesh['px'=32,'py'=8] {'px'}, dimensions={0} | all-to-all | bytes 65536 | tf_op jit(solution)/shard_map/all_to_all | solution.py:66
  336.8 13.1 %all_to_all.403 = f32[8,1,1024]{2,1,0:T(1,128)S(1)} all-to-all(f32[8,1,1024]{2,1,0:T(1,128)S(1)} %reshape.126), channel_id=1, replica_groups=mesh['px'=32,'py'=8] {'py'}, dimensions={0} | all-to-all | bytes 65536 | tf_op jit(solution)/shard_map/all_to_all | solution.py:67
  357.3 10.2 %all_to_all.404 = f32[8,1,1024]{2,1,0:T(1,128)S(1)} all-to-all(f32[8,1,1024]{2,1,0:T(1,128)S(1)} %reshape.128), channel_id=1, replica_groups=mesh['px'=32,'py'=8] {'py'}, dimensions={0} | all-to-all | bytes 65536 | tf_op jit(solution)/shard_map/all_to_all | solution.py:56
  379.4 5.6 all-to-all-done.19
  384.9 5.7 all-to-all-start
  392.1 6.3 bitcast_subtract_fusion.1
  398.8 6.2 log_add_fusion.4
  405.9 3.9 all-to-all-start.20
  412.2 4.7 all-to-all-done.20
  422.9 8.6 %all-to-all-start.21 = ((f32[8,1,1024]{2,1,0:T(1,128)}), f32[8,1,1024]{2,1,0:T(1,128)S(1)}, u32[]{:S(2)}, u32[]{:S(2)}) async-start(f32[8,1,1024]{2,1,0:T(1,128)} %reshape.134), calls=%async_computation.21 | async-start | bytes 65536 | tf_op jit(solution)/shard_map/all_to_all | solution.py:67
  431.5 7.1 %all-to-all-done.21 = f32[8,1,1024]{2,1,0:T(1,128)S(1)} async-done(((f32[8,1,1024]{2,1,0:T(1,128)}), f32[8,1,1024]{2,1,0:T(1,128)S(1)}, u32[]{:S(2)}, u32[]{:S(2)}) %all-to-all-start.21) | async-done | bytes 32800 | tf_op jit(solution)/shard_map/all_to_all | solution.py:67
  443.5 9.6 %reduce_window_max.288 = f32[8,32,256]{2,1,0:T(8,128)S(1)} reduce-window(f32[8,32,256]{2,1,0:T(8,128)S(1)} %copy.467, f32[]{:T(128)} %constant.46.clone.1), window={size=1x1x33 pad=0_0x0_0x16_16}, to_apply=%region_31.32 | reduce-window | flops 2097152 | bytes 524292 | tf_op jit(solution)/shard_map/reduce_window_max | solution.py:24
  458.8 4.0 all-to-all-start.22
  464.0 9.0 %all-to-all-done.22 = f32[8,1,8192]{2,1,0:T(1,128)S(1)} async-done(((f32[8,1,8192]{2,1,0:T(1,128)}), f32[8,1,8192]{2,1,0:T(1,128)S(1)}, u32[]{:S(2)}, u32[]{:S(2)}) %all-to-all-start.22) | async-done | bytes 262176 | tf_op jit(solution)/shard_map/all_to_all | solution.py:56
  473.1 3.9 all-to-all-start.1
  479.1 18.9 %fusion.2787 = f32[8,256,32]{2,0,1:T(8,128)S(1)} fusion(f32[8,256,32]{2,0,1:T(8,128)S(1)} %bitcast.1243), kind=kOutput, calls=%fused_computation.4066 | output fusion | flops 2097152 | bytes 524288 | tf_op jit(solution)/shard_map/reduce_window_max | solution.py:24
  497.9 11.8 %log_add_fusion.2 = f32[8,256,32]{2,0,1:T(8,128)S(1)} fusion(f32[8,256,32]{2,0,1:T(8,128)S(1)} %fusion.2787, f32[8,256,32]{2,0,1:T(8,128)S(1)} %bitcast.1244), kind=kLoop, calls=%fused_computation.523 | loop fusion | flops 6422528 | bytes 786432 | tf_op jit(solution)/shard_map/add | solution.py:34
  511.3 8.0 %all-to-all-start.23 = ((f32[32,1,2048]{2,1,0:T(1,128)}), f32[32,1,2048]{2,1,0:T(1,128)S(1)}, u32[]{:S(2)}, u32[]{:S(2)}) async-start(f32[32,1,2048]{2,1,0:T(1,128)} %reshape.138), calls=%async_computation.23 | async-start | bytes 524288 | tf_op jit(solution)/shard_map/all_to_all | solution.py:59
  520.9 6.2 all-to-all-done.23
  529.0 18.9 %fusion.2788 = f32[256,8,32]{2,1,0:T(8,128)S(1)} fusion(f32[256,8,32]{2,1,0:T(8,128)S(1)} %bitcast.1197), kind=kOutput, calls=%fused_computation.4067 | output fusion | flops 2097152 | bytes 524288 | tf_op jit(solution)/shard_map/reduce_window_max | solution.py:24
  547.9 11.9 %broadcast_multiply_fusion = (f32[256,8,32]{2,1,0:T(8,128)S(1)}, f32[256,8,32]{2,1,0:T(8,128)S(1)}) fusion(f32[256,8,32]{2,1,0:T(8,128)S(1)} %fusion.2788, f32[256,8,32]{2,1,0:T(8,128)S(1)} %bitcast.1198, f32[32,8,8,32]{3,2,1,0:T(8,128)S(1)} %reshape.105), kind=kLoop, calls=%fused_computation.1058 | loop fusion | flops 6553600 | bytes 1310720 | tf_op jit(solution)/shard_map/mul | solution.py:81
  561.0 3.9 all-to-all-start.24
  564.9 18.9 %fusion.2789 = f32[256,8,32]{2,1,0:T(8,128)S(1)} fusion(f32[256,8,32]{2,1,0:T(8,128)S(1)} %get-tuple-element.3), kind=kOutput, calls=%fused_computation.4068 | output fusion | flops 2097152 | bytes 524288 | tf_op jit(solution)/shard_map/reduce_window_max | solution.py:24
  583.7 11.8 %log_add_fusion.1 = f32[256,8,32]{2,1,0:T(8,128)S(1)} fusion(f32[256,8,32]{2,1,0:T(8,128)S(1)} %fusion.2789, f32[256,8,32]{2,1,0:T(8,128)S(1)} %get-tuple-element.3), kind=kLoop, calls=%fused_computation.222 | loop fusion | flops 6422528 | bytes 786432 | tf_op jit(solution)/shard_map/add | solution.py:34
  596.7 7.8 %all-to-all-start.26 = ((f32[32,1,2048]{2,1,0:T(1,128)}), f32[32,1,2048]{2,1,0:T(1,128)S(1)}, u32[]{:S(2)}, u32[]{:S(2)}) async-start(f32[32,1,2048]{2,1,0:T(1,128)} %reshape.144), calls=%async_computation.26 | async-start | bytes 524288 | tf_op jit(solution)/shard_map/all_to_all | solution.py:66
  608.0 4.4 all-to-all-done.26
  612.3 9.3 %all-to-all-start.25 = ((f32[8,1,8192]{2,1,0:T(1,128)}), f32[8,1,8192]{2,1,0:T(1,128)S(1)}, u32[]{:S(2)}, u32[]{:S(2)}) async-start(f32[8,1,8192]{2,1,0:T(1,128)} %reshape.142), calls=%async_computation.25 | async-start | bytes 524288 | tf_op jit(solution)/shard_map/all_to_all | solution.py:67
  623.5 18.9 %fusion.2790 = f32[8,256,32]{2,0,1:T(8,128)S(1)} fusion(f32[8,256,32]{2,0,1:T(8,128)S(1)} %bitcast.1245), kind=kOutput, calls=%fused_computation.4069 | output fusion | flops 2097152 | bytes 524288 | tf_op jit(solution)/shard_map/reduce_window_max | solution.py:24
  642.4 11.8 %fusion.2778 = f32[256,8,32]{2,1,0:T(8,128)S(1)} fusion(f32[8,256,32]{2,0,1:T(8,128)S(1)} %fusion.2790, f32[8,256,32]{2,0,1:T(8,128)S(1)} %bitcast.1246), kind=kLoop, calls=%fused_computation.4052 | loop fusion | flops 6422528 | bytes 786432
  655.3 7.2 %all-to-all-start.27 = ((f32[8,1,8192]{2,1,0:T(1,128)}), f32[8,1,8192]{2,1,0:T(1,128)S(1)}, u32[]{:S(2)}, u32[]{:S(2)}) async-start(f32[8,1,8192]{2,1,0:T(1,128)} %reshape.146), calls=%async_computation.27 | async-start | bytes 524288 | tf_op jit(solution)/shard_map/all_to_all | solution.py:67
  665.8 6.8 all-to-all-done.27
  675.2 9.6 %reduce_window_max.293 = f32[8,32,256]{2,1,0:T(8,128)S(1)} reduce-window(f32[8,32,256]{2,1,0:T(8,128)S(1)} %all_to_all.371, f32[]{:T(128)} %constant.46.clone.1), window={size=1x1x33 pad=0_0x0_0x16_16}, to_apply=%region_36.37 | reduce-window | flops 2097152 | bytes 524292 | tf_op jit(solution)/shard_map/reduce_window_max | solution.py:24
  (449 shorter events, 161.3 us)
Async XLA Ops:
  36.8 11.7 %copy-start.3 = (f32[8,32,256]{2,1,0:T(8,128)S(1)}, f32[8,32,256]{2,1,0:T(8,128)}, u32[]{:S(2)}) copy-start(f32[8,32,256]{2,1,0:T(8,128)} %param.3) | copy-start | bytes 786436
  38.5 44.3 %all-to-all-start.4 = ((f32[8,1,128]{2,1,0:T(1,128)}), f32[8,1,128]{2,1,0:T(1,128)S(1)}, u32[]{:S(2)}, u32[]{:S(2)}) async-start(f32[8,1,128]{2,1,0:T(1,128)} %reshape.110), calls=%async_computation.4 | async-start | bytes 8192 | tf_op jit(solution)/shard_map/all_to_all | solution.py:56
  82.8 26.8 %all-to-all-start.6 = ((f32[8,1,128]{2,1,0:T(1,128)}), f32[8,1,128]{2,1,0:T(1,128)S(1)}, u32[]{:S(2)}, u32[]{:S(2)}) async-start(f32[8,1,128]{2,1,0:T(1,128)} %reshape.112), calls=%async_computation.6 | async-start | bytes 8192 | tf_op jit(solution)/shard_map/all_to_all | solution.py:56
  130.0 14.8 %all-to-all-start.7 = ((f32[32,2,2,8]{3,2,1,0:T(2,128)}), f32[32,2,2,8]{3,2,1,0:T(2,128)S(1)}, u32[]{:S(2)}, u32[]{:S(2)}) async-start(f32[32,2,2,8]{3,2,1,0:T(2,128)} %constant_dynamic-update-slice_fusion.96), calls=%async_computation.7 | async-start | bytes 131072 | tf_op jit(solution)/shard_map/all_to_all | solution.py:59
  144.8 11.0 %all-to-all-start.5 = ((f32[32,2,2,8]{3,2,1,0:T(2,128)}), f32[32,2,2,8]{3,2,1,0:T(2,128)S(1)}, u32[]{:S(2)}, u32[]{:S(2)}) async-start(f32[32,2,2,8]{3,2,1,0:T(2,128)} %constant_dynamic-update-slice_fusion.64), calls=%async_computation.5 | async-start | bytes 131072 | tf_op jit(solution)/shard_map/all_to_all | solution.py:59
  163.4 11.0 %all-to-all-start.8 = ((f32[64,2,8]{2,1,0:T(2,128)}), f32[64,2,8]{2,1,0:T(2,128)S(1)}, u32[]{:S(2)}, u32[]{:S(2)}) async-start(f32[64,2,8]{2,1,0:T(2,128)} %log_add_fusion.10), calls=%async_computation.8 | async-start | bytes 131072 | tf_op jit(solution)/shard_map/all_to_all | solution.py:66
  176.2 17.8 %all-to-all-start.9 = ((f32[8,1,128]{2,1,0:T(1,128)}), f32[8,1,128]{2,1,0:T(1,128)S(1)}, u32[]{:S(2)}, u32[]{:S(2)}) async-start(f32[8,1,128]{2,1,0:T(1,128)} %reshape.114), calls=%async_computation.9 | async-start | bytes 8192 | tf_op jit(solution)/shard_map/all_to_all | solution.py:67
  227.9 11.0 %all-to-all-start.12 = ((f32[64,2,8]{2,1,0:T(2,128)}), f32[64,2,8]{2,1,0:T(2,128)S(1)}, u32[]{:S(2)}, u32[]{:S(2)}) async-start(f32[64,2,8]{2,1,0:T(2,128)} %log_add_fusion.7), calls=%async_computation.12 | async-start | bytes 131072 | tf_op jit(solution)/shard_map/all_to_all | solution.py:66
  238.9 13.7 %all-to-all-start.2 = ((f32[8,1,1024]{2,1,0:T(1,128)}), f32[8,1,1024]{2,1,0:T(1,128)S(1)}, u32[]{:S(2)}, u32[]{:S(2)}) async-start(f32[8,1,1024]{2,1,0:T(1,128)} %reshape.106), calls=%async_computation.2 | async-start | bytes 65536 | tf_op jit(solution)/shard_map/all_to_all | solution.py:56
  252.6 10.9 %all-to-all-start.13 = ((f32[8,1,128]{2,1,0:T(1,128)}), f32[8,1,128]{2,1,0:T(1,128)S(1)}, u32[]{:S(2)}, u32[]{:S(2)}) async-start(f32[8,1,128]{2,1,0:T(1,128)} %reshape.118), calls=%async_computation.13 | async-start | bytes 8192 | tf_op jit(solution)/shard_map/all_to_all | solution.py:67
  269.5 11.1 %all-to-all-start.14 = ((f32[8,1,1024]{2,1,0:T(1,128)}), f32[8,1,1024]{2,1,0:T(1,128)S(1)}, u32[]{:S(2)}, u32[]{:S(2)}) async-start(f32[8,1,1024]{2,1,0:T(1,128)} %reshape.120), calls=%async_computation.14 | async-start | bytes 65536 | tf_op jit(solution)/shard_map/all_to_all | solution.py:56
  280.6 11.2 %all-to-all-start.3 = ((f32[32,1,256]{2,1,0:T(1,128)}), f32[32,1,256]{2,1,0:T(1,128)S(1)}, u32[]{:S(2)}, u32[]{:S(2)}) async-start(f32[32,1,256]{2,1,0:T(1,128)} %reshape.108), calls=%async_computation.3 | async-start | bytes 65536 | tf_op jit(solution)/shard_map/all_to_all | solution.py:59
  291.7 14.3 %all-to-all-start.15 = ((f32[32,1,256]{2,1,0:T(1,128)}), f32[32,1,256]{2,1,0:T(1,128)S(1)}, u32[]{:S(2)}, u32[]{:S(2)}) async-start(f32[32,1,256]{2,1,0:T(1,128)} %reshape.122), calls=%async_computation.15 | async-start | bytes 65536 | tf_op jit(solution)/shard_map/all_to_all | solution.py:59
  356.5 21.2 %copy-start.2 = (f32[8,32,256]{2,1,0:T(8,128)S(1)}, f32[8,32,256]{2,1,0:T(8,128)}, u32[]{:S(2)}) copy-start(f32[8,32,256]{2,1,0:T(8,128)} %param.2) | copy-start | bytes 786436
  373.9 11.0 %all-to-all-start.19 = ((f32[32,1,256]{2,1,0:T(1,128)}), f32[32,1,256]{2,1,0:T(1,128)S(1)}, u32[]{:S(2)}, u32[]{:S(2)}) async-start(f32[32,1,256]{2,1,0:T(1,128)} %reshape.130), calls=%async_computation.19 | async-start | bytes 65536 | tf_op jit(solution)/shard_map/all_to_all | solution.py:59
  384.9 20.9 %all-to-all-start = ((f32[8,1,8192]{2,1,0:T(1,128)}), f32[8,1,8192]{2,1,0:T(1,128)S(1)}, u32[]{:S(2)}, u32[]{:S(2)}) async-start(f32[8,1,8192]{2,1,0:T(1,128)} %reshape.102), calls=%async_computation | async-start | bytes 524288 | tf_op jit(solution)/shard_map/all_to_all | solution.py:56
  405.9 11.0 %all-to-all-start.20 = ((f32[32,1,256]{2,1,0:T(1,128)}), f32[32,1,256]{2,1,0:T(1,128)S(1)}, u32[]{:S(2)}, u32[]{:S(2)}) async-start(f32[32,1,256]{2,1,0:T(1,128)} %reshape.132), calls=%async_computation.20 | async-start | bytes 65536 | tf_op jit(solution)/shard_map/all_to_all | solution.py:66
  422.9 15.7 %all-to-all-start.21 = ((f32[8,1,1024]{2,1,0:T(1,128)}), f32[8,1,1024]{2,1,0:T(1,128)S(1)}, u32[]{:S(2)}, u32[]{:S(2)}) async-start(f32[8,1,1024]{2,1,0:T(1,128)} %reshape.134), calls=%async_computation.21 | async-start | bytes 65536 | tf_op jit(solution)/shard_map/all_to_all | solution.py:67
  431.5 11.3 %copy-start = (f32[32,8,8,32]{3,2,1,0:T(8,128)}, f32[32,8,8,32]{3,2,1,0:T(8,128)S(1)}, u32[]{:S(2)}) copy-start(f32[32,8,8,32]{3,2,1,0:T(8,128)S(1)} %constant_dynamic-update-slice_fusion.3) | copy-start | bytes 786436
  456.2 6.7 copy-start.1
  458.8 14.3 %all-to-all-start.22 = ((f32[8,1,8192]{2,1,0:T(1,128)}), f32[8,1,8192]{2,1,0:T(1,128)S(1)}, u32[]{:S(2)}, u32[]{:S(2)}) async-start(f32[8,1,8192]{2,1,0:T(1,128)} %reshape.136), calls=%async_computation.22 | async-start | bytes 524288 | tf_op jit(solution)/shard_map/all_to_all | solution.py:56
  473.1 38.2 %all-to-all-start.1 = ((f32[32,1,2048]{2,1,0:T(1,128)}), f32[32,1,2048]{2,1,0:T(1,128)S(1)}, u32[]{:S(2)}, u32[]{:S(2)}) async-start(f32[32,1,2048]{2,1,0:T(1,128)} %reshape.104), calls=%async_computation.1 | async-start | bytes 524288 | tf_op jit(solution)/shard_map/all_to_all | solution.py:59
  511.3 15.9 %all-to-all-start.23 = ((f32[32,1,2048]{2,1,0:T(1,128)}), f32[32,1,2048]{2,1,0:T(1,128)S(1)}, u32[]{:S(2)}, u32[]{:S(2)}) async-start(f32[32,1,2048]{2,1,0:T(1,128)} %reshape.138), calls=%async_computation.23 | async-start | bytes 524288 | tf_op jit(solution)/shard_map/all_to_all | solution.py:59
  561.0 35.7 %all-to-all-start.24 = ((f32[32,1,2048]{2,1,0:T(1,128)}), f32[32,1,2048]{2,1,0:T(1,128)S(1)}, u32[]{:S(2)}, u32[]{:S(2)}) async-start(f32[32,1,2048]{2,1,0:T(1,128)} %reshape.140), calls=%async_computation.24 | async-start | bytes 524288 | tf_op jit(solution)/shard_map/all_to_all | solution.py:66
  596.7 15.7 %all-to-all-start.26 = ((f32[32,1,2048]{2,1,0:T(1,128)}), f32[32,1,2048]{2,1,0:T(1,128)S(1)}, u32[]{:S(2)}, u32[]{:S(2)}) async-start(f32[32,1,2048]{2,1,0:T(1,128)} %reshape.144), calls=%async_computation.26 | async-start | bytes 524288 | tf_op jit(solution)/shard_map/all_to_all | solution.py:66
  612.3 42.9 %all-to-all-start.25 = ((f32[8,1,8192]{2,1,0:T(1,128)}), f32[8,1,8192]{2,1,0:T(1,128)S(1)}, u32[]{:S(2)}, u32[]{:S(2)}) async-start(f32[8,1,8192]{2,1,0:T(1,128)} %reshape.142), calls=%async_computation.25 | async-start | bytes 524288 | tf_op jit(solution)/shard_map/all_to_all | solution.py:67
  655.3 17.3 %all-to-all-start.27 = ((f32[8,1,8192]{2,1,0:T(1,128)}), f32[8,1,8192]{2,1,0:T(1,128)S(1)}, u32[]{:S(2)}, u32[]{:S(2)}) async-start(f32[8,1,8192]{2,1,0:T(1,128)} %reshape.146), calls=%async_computation.27 | async-start | bytes 524288 | tf_op jit(solution)/shard_map/all_to_all | solution.py:67
